TPU v7x, 32 devices: a whole 2x2x4 slice. The times are simulated.
32 devices in a mesh: section: 2 (over y), expert: 16 (over z, x, core).
Axes of the slice: x: 2, y: 2, z: 4, core: 2. Of those that a mesh axis runs over, the one named last changes fastest.
Arguments:
- inputs: bfloat16 [2, 256, 2560], P('section', 'expert'), may hold values from -6 to 6
- norm_gain: float32 [2, 2, 2560], P(None, 'section'), may hold values from 0.5 to 1.5
- router: bfloat16 [2, 2, 2560, 16], P(None, 'section'), may hold values from -0.125 to 0.125
- w_gate: bfloat16 [2, 2, 16, 2560, 768], P(None, 'section', 'expert'), may hold values from -0.125 to 0.125
- w_up: bfloat16 [2, 2, 16, 2560, 768], P(None, 'section', 'expert'), may hold values from -0.125 to 0.125
- w_down: bfloat16 [2, 2, 16, 768, 2560], P(None, 'section', 'expert'), may hold values from -0.21875 to 0.21875
- routes: int32 [2, 2, 2, 256, 6], P(None, 'section'), may hold values from 0 to 15, all different within a row; in each aligned block of 16 rows (0 to 15, 16 to 31, ..., all dimensions but the last counted through in order) at most 9 rows name the same one
Outputs:
- outputs: bfloat16 [2, 256, 2560], P('section', 'expert')
Inputs may be any that keep to these rules, and one draw needn't show every extreme that they name: Each row names 6 different experts. In each aligned block of 16 rows of routes (the tokens of one index of expert in one micro-batch at one layer), no expert is named by more than 9 rows.
All inputs are finite; a program needn't handle non-finite values.
Results may differ from a plain program's by a relative error of at most 0.012.
Values may be sent and summed in bfloat16 or wider, within the bound.
A program may use at most 64 MiB of HBM per device.

v0:
```python
import jax
import jax.numpy as jnp
from jax import lax
from jax.sharding import PartitionSpec as P


def passed_along(array, axis, by):
    size = lax.axis_size(axis)
    return lax.ppermute(array, axis, [(i, (i + by) % size) for i in range(size)])


def passed_along_2(block, axis, distance):
    devices = range(lax.axis_size(axis))
    route = [(i - distance, i) for i in devices if i - distance in devices]
    return lax.ppermute(block, axis, route)


def normalize(values, gain_row):
    wide = values.astype(jnp.float32)
    scale = lax.rsqrt(jnp.mean(wide * wide, axis=-1, keepdims=True) + 1e-06)
    return (wide * scale * gain_row).astype(jnp.bfloat16)


def gate_weights(normed, router_now, routes_rows):
    scores = jnp.dot(normed, router_now, preferred_element_type=jnp.float32)
    expert_ids = lax.broadcasted_iota(jnp.int32, (1, 1, router_now.shape[1]), 2)
    onehot = (routes_rows[:, :, None] == expert_ids).astype(jnp.float32)
    picked = jnp.sum(onehot * scores[:, None, :], axis=2)
    sigmoid_of = jax.nn.sigmoid(picked)
    return sigmoid_of / jnp.sum(sigmoid_of, axis=1, keepdims=True)


def slot_table(routes_rows, slab_rows, experts):
    top_k = routes_rows.shape[1]
    blocks = routes_rows.reshape(-1, slab_rows * top_k)
    expert_ids = lax.broadcasted_iota(jnp.int32, (1, 1, experts), 2)
    onehot = (blocks[:, :, None] == expert_ids).astype(jnp.int32)
    before = jnp.cumsum(onehot, axis=1) - onehot
    return jnp.sum(before * onehot, axis=2).reshape(routes_rows.shape)


def expert_rows(rows_in, gate_mat, up_mat, down_mat):
    gate_proj = jnp.dot(rows_in, gate_mat, preferred_element_type=jnp.float32)
    up_proj = jnp.dot(rows_in, up_mat, preferred_element_type=jnp.float32)
    hidden = (jax.nn.silu(gate_proj) * up_proj).astype(jnp.bfloat16)
    return jnp.dot(hidden, down_mat, preferred_element_type=jnp.float32).astype(jnp.bfloat16)


def weighted_rows(weights, values):
    upper = weights.astype(jnp.bfloat16)
    lower = (weights - upper.astype(jnp.float32)).astype(jnp.bfloat16)
    first = jnp.dot(upper, values, preferred_element_type=jnp.float32)
    return first + jnp.dot(lower, values, preferred_element_type=jnp.float32)


def per_device(inputs, norm_gain, router, w_gate, w_up, w_down, routes):
    sections = lax.axis_size("section")
    section_at = lax.axis_index("section")
    owner_at = lax.axis_index("expert")
    slab_rows = inputs.shape[1]
    feature = inputs.shape[2]
    experts = router.shape[3]
    top_k = routes.shape[4]
    capacity = min(slab_rows, 3 * slab_rows * top_k // (2 * experts))
    step_count = 3 * sections - 1
    positions = lax.broadcasted_iota(jnp.int32, (1, 1, experts * capacity), 2)

    def layer(slab_in, moment):
        offset = moment - section_at
        is_busy = (offset >= 0) & (offset < 2 * sections)
        clipped = jnp.clip(offset, 0, 2 * sections - 1)
        loop_at = clipped // sections
        micro_at = clipped % sections
        gain_row = lax.dynamic_index_in_dim(norm_gain[:, 0], loop_at, 0, keepdims=False)
        router_now = lax.dynamic_index_in_dim(router[:, 0], loop_at, 0, keepdims=False)
        gate_mat = lax.dynamic_index_in_dim(w_gate[:, 0, 0], loop_at, 0, keepdims=False)
        up_mat = lax.dynamic_index_in_dim(w_up[:, 0, 0], loop_at, 0, keepdims=False)
        down_mat = lax.dynamic_index_in_dim(w_down[:, 0, 0], loop_at, 0, keepdims=False)
        routes_loop = lax.dynamic_index_in_dim(routes[:, 0], loop_at, 0, keepdims=False)
        routes_now = lax.dynamic_index_in_dim(routes_loop, micro_at, 0, keepdims=False)
        normed = normalize(slab_in, gain_row)
        own_routes = lax.dynamic_slice_in_dim(routes_now, owner_at * slab_rows, slab_rows, 0)
        gates = gate_weights(normed, router_now, own_routes)
        slots = slot_table(own_routes, slab_rows, experts)
        placed = own_routes * capacity + slots
        matches = placed[:, :, None] == positions
        select = jnp.any(matches, axis=1).astype(jnp.bfloat16)
        combine = jnp.sum(jnp.where(matches, gates[:, :, None], 0.0), axis=1)
        sending = jnp.einsum(
            "rp,rd->pd", select, normed, preferred_element_type=jnp.float32
        ).astype(jnp.bfloat16)
        sending = sending.reshape(experts, capacity, feature)
        received = lax.all_to_all(sending, "expert", split_axis=0, concat_axis=0, tiled=True)
        answered = lax.cond(
            is_busy,
            lambda values: expert_rows(values, gate_mat, up_mat, down_mat),
            jnp.zeros_like,
            received.reshape(-1, feature),
        ).reshape(received.shape)
        returned = lax.all_to_all(answered, "expert", split_axis=0, concat_axis=0, tiled=True)
        mixed = weighted_rows(combine, returned.reshape(-1, feature))
        return ((slab_in.astype(jnp.float32) + mixed).astype(jnp.bfloat16), micro_at)

    empty_slab = jnp.zeros_like(inputs[0])
    initial = (empty_slab, inputs[0], empty_slab)

    def advance(moment, loop_state):
        carried, feed_box, outbox = loop_state
        entering = (section_at == 0) & (moment < sections)
        fresh = feed_box
        slab_in = jnp.where(entering, fresh, carried)
        result, micro_at = layer(slab_in, moment)
        carried = passed_along(result, "section", 1)
        finish = (section_at == sections - 1) & (moment >= 2 * sections - 1)
        feed_box, outbox = passed_along_2((feed_box, outbox), "section", -1)
        outbox = jnp.where(finish, result, outbox)
        return (carried, feed_box, outbox)

    loop_state = lax.fori_loop(0, step_count, advance, initial)
    return loop_state[2][None]


def solution(mesh):
    return jax.shard_map(
        per_device,
        mesh=mesh,
        in_specs=(
            P("section", "expert", None),
            P(None, "section", None),
            P(None, "section", None, None),
            P(None, "section", "expert", None, None),
            P(None, "section", "expert", None, None),
            P(None, "section", "expert", None, None),
            P(None, "section", None, None, None),
        ),
        out_specs=P("section", "expert", None),
        check_vma=False,
    )
```

profile of v0, /device:TPU:20, one launch (start us, length us, event | category | flops | bytes accessed | tf_op | source)
XLA Modules:
  0.0 453.2 jit_solution(15295944289878618531)
XLA Ops:
  0.9 451.7 %while.21 = (s32[]{:T(128)}, bf16[16,2560]{1,0:T(8,128)(2,1)S(1)}, bf16[16,2560]{1,0:T(8,128)(2,1)S(1)}, bf16[16,2560]{1,0:T(8,128)(2,1)S(1)}, pred[]{:T(512)}, ...) while((s32[]{:T(128)}, bf16[16,2560]{1,0:T(8,128)(2,1)S(1)}, ...), condition=%wide.region_10.11_spmd.clone, body=%wide.region_0.10_spmd.clone.sunk | while | flops 1737769472 | bytes 32948616 | solution.py:119
  5.3 6.2 %all-to-all-start = ((bf16[16,9,2560]{2,1,0:T(8,128)(2,1)}), bf16[16,9,2560]{2,1,0:T(8,128)(2,1)S(1)}, u32[]{:S(2)}, u32[]{:S(2)}) async-start(bf16[16,9,2560]{2,1,0:T(8,128)(2,1)} %reshape.244), calls=%async_computation | async-start | bytes 2621440 | tf_op jit(solution)/shard_map/while/body/eval_jaxpr/all_to_all | solution.py:93
  13.8 28.4 %all-to-all-done = bf16[16,9,2560]{2,1,0:T(8,128)(2,1)S(1)} async-done(((bf16[16,9,2560]{2,1,0:T(8,128)(2,1)}), bf16[16,9,2560]{2,1,0:T(8,128)(2,1)S(1)}, u32[]{:S(2)}, u32[]{:S(2)}) %all-to-all-start) | async-done | bytes 737312 | tf_op jit(solution)/shard_map/while/body/eval_jaxpr/all_to_all | solution.py:93
  43.7 4.6 %all-to-all-start.1 = ((bf16[16,9,2560]{2,1,0:T(8,128)(2,1)}), bf16[16,9,2560]{2,1,0:T(8,128)(2,1)S(1)}, u32[]{:S(2)}, u32[]{:S(2)}) async-start(bf16[16,9,2560]{2,1,0:T(8,128)(2,1)} %reshape.245), calls=%async_computation.1 | async-start | bytes 2621440 | tf_op jit(solution)/shard_map/while/body/eval_jaxpr/all_to_all | solution.py:100
  48.3 10.6 %collective-permute-start = (bf16[16,2560]{1,0:T(8,128)(2,1)S(1)}, bf16[16,2560]{1,0:T(8,128)(2,1)S(1)}, u32[]{:S(2)}, u32[]{:S(2)}) collective-permute-start(bf16[16,2560]{1,0:T(8,128)(2,1)S(1)} %broadcast_select_fusion.6), channel_id=1, source_target_pairs={{16,0},{17,1},{18,2},{19,3},{20,4},{21,5},{22,6},{23,7},{24,8},{25... | collective-permute-start | bytes 245768 | tf_op jit(solution)/shard_map/while/body/eval_jaxpr/ppermute | solution.py:15
  59.5 19.6 %all-to-all-done.1 = bf16[16,9,2560]{2,1,0:T(8,128)(2,1)S(1)} async-done(((bf16[16,9,2560]{2,1,0:T(8,128)(2,1)}), bf16[16,9,2560]{2,1,0:T(8,128)(2,1)S(1)}, u32[]{:S(2)}, u32[]{:S(2)}) %all-to-all-start.1) | async-done | bytes 737312 | tf_op jit(solution)/shard_map/while/body/eval_jaxpr/all_to_all | solution.py:100
  79.8 8.8 %collective-permute-start.1 = (bf16[16,2560]{1,0:T(8,128)(2,1)S(1)}, bf16[16,2560]{1,0:T(8,128)(2,1)S(1)}, u32[]{:S(2)}, u32[]{:S(2)}) collective-permute-start(bf16[16,2560]{1,0:T(8,128)(2,1)S(1)} %get-tuple-element.674), channel_id=1, source_target_pairs={{0,16},{16,0},{1,17},{17,1},{2,18},{18,2},{3,19},{19,3},{4,20},{20... | collective-permute-start | bytes 245768 | tf_op jit(solution)/shard_map/while/body/eval_jaxpr/ppermute | solution.py:9
  95.4 5.1 %all-to-all-start = ((bf16[16,9,2560]{2,1,0:T(8,128)(2,1)}), bf16[16,9,2560]{2,1,0:T(8,128)(2,1)S(1)}, u32[]{:S(2)}, u32[]{:S(2)}) async-start(bf16[16,9,2560]{2,1,0:T(8,128)(2,1)} %reshape.244), calls=%async_computation | async-start | bytes 2621440 | tf_op jit(solution)/shard_map/while/body/eval_jaxpr/all_to_all | solution.py:93
  104.2 27.1 %all-to-all-done = bf16[16,9,2560]{2,1,0:T(8,128)(2,1)S(1)} async-done(((bf16[16,9,2560]{2,1,0:T(8,128)(2,1)}), bf16[16,9,2560]{2,1,0:T(8,128)(2,1)S(1)}, u32[]{:S(2)}, u32[]{:S(2)}) %all-to-all-start) | async-done | bytes 737312 | tf_op jit(solution)/shard_map/while/body/eval_jaxpr/all_to_all | solution.py:93
  131.3 8.3 %conditional.3 = (bf16[144,2560]{1,0:T(8,128)(2,1)S(1)}) conditional(s32[]{:T(128)} %convert_element_type.207, () %tuple.69, (bf16[2,1,1,2560,768]{4,3,2,1,0:T(8,128)(2,1)}, s32[]{:T(128)}, bf16[16,9,2560]{2,1,0:T(8,128)(2,1)S(1)}, bf16[2,1,1,2560,768]{4,3,2,1,0:T(8,128)(2,1)}, bf16[2,1,1,768,2560]{4,3,2,1,0:T(8,128)(2,1)}) %tuple.70), branch_computations={%region_8.8_spmd, %region_9.9_spmd} | conditional | flops 1699725312 | bytes 16369160 | solution.py:94
  134.5 5.1 %fusion.11 = bf16[144,2560]{1,0:T(8,128)(2,1)S(1)} fusion(bf16[2,1,1,768,2560]{4,3,2,1,0:T(8,128)(2,1)} %get-tuple-element.443, s32[]{:T(128)} %get-tuple-element.440, bf16[144,2560]{1,0:T(8,128)(2,1)S(1)} %reshape.229, bf16[2,1,1,2560,768]{4,3,2,1,0:T(8,128)(2,1)} %get-tuple-element.442, f32[144,768]{1,0:T(8,128)S(1)} %fusion.14), kind=kOutput, calls=%fused_computation.10 | convolution fusion | flops 1133494272 | bytes 9782272 | tf_op jit(solution)/shard_map/while/body/eval_jaxpr/cond/branch_1_fun/dot_general | solution.py:46
  140.9 4.6 %all-to-all-start.1 = ((bf16[16,9,2560]{2,1,0:T(8,128)(2,1)}), bf16[16,9,2560]{2,1,0:T(8,128)(2,1)S(1)}, u32[]{:S(2)}, u32[]{:S(2)}) async-start(bf16[16,9,2560]{2,1,0:T(8,128)(2,1)} %reshape.245), calls=%async_computation.1 | async-start | bytes 2621440 | tf_op jit(solution)/shard_map/while/body/eval_jaxpr/all_to_all | solution.py:100
  149.8 26.5 %all-to-all-done.1 = bf16[16,9,2560]{2,1,0:T(8,128)(2,1)S(1)} async-done(((bf16[16,9,2560]{2,1,0:T(8,128)(2,1)}), bf16[16,9,2560]{2,1,0:T(8,128)(2,1)S(1)}, u32[]{:S(2)}, u32[]{:S(2)}) %all-to-all-start.1) | async-done | bytes 737312 | tf_op jit(solution)/shard_map/while/body/eval_jaxpr/all_to_all | solution.py:100
  186.0 4.8 %all-to-all-start = ((bf16[16,9,2560]{2,1,0:T(8,128)(2,1)}), bf16[16,9,2560]{2,1,0:T(8,128)(2,1)S(1)}, u32[]{:S(2)}, u32[]{:S(2)}) async-start(bf16[16,9,2560]{2,1,0:T(8,128)(2,1)} %reshape.244), calls=%async_computation | async-start | bytes 2621440 | tf_op jit(solution)/shard_map/while/body/eval_jaxpr/all_to_all | solution.py:93
  194.5 27.1 %all-to-all-done = bf16[16,9,2560]{2,1,0:T(8,128)(2,1)S(1)} async-done(((bf16[16,9,2560]{2,1,0:T(8,128)(2,1)}), bf16[16,9,2560]{2,1,0:T(8,128)(2,1)S(1)}, u32[]{:S(2)}, u32[]{:S(2)}) %all-to-all-start) | async-done | bytes 737312 | tf_op jit(solution)/shard_map/while/body/eval_jaxpr/all_to_all | solution.py:93
  221.6 8.3 %conditional.3 = (bf16[144,2560]{1,0:T(8,128)(2,1)S(1)}) conditional(s32[]{:T(128)} %convert_element_type.207, () %tuple.69, (bf16[2,1,1,2560,768]{4,3,2,1,0:T(8,128)(2,1)}, s32[]{:T(128)}, bf16[16,9,2560]{2,1,0:T(8,128)(2,1)S(1)}, bf16[2,1,1,2560,768]{4,3,2,1,0:T(8,128)(2,1)}, bf16[2,1,1,768,2560]{4,3,2,1,0:T(8,128)(2,1)}) %tuple.70), branch_computations={%region_8.8_spmd, %region_9.9_spmd} | conditional | flops 1699725312 | bytes 16369160 | solution.py:94
  224.8 5.1 %fusion.11 = bf16[144,2560]{1,0:T(8,128)(2,1)S(1)} fusion(bf16[2,1,1,768,2560]{4,3,2,1,0:T(8,128)(2,1)} %get-tuple-element.443, s32[]{:T(128)} %get-tuple-element.440, bf16[144,2560]{1,0:T(8,128)(2,1)S(1)} %reshape.229, bf16[2,1,1,2560,768]{4,3,2,1,0:T(8,128)(2,1)} %get-tuple-element.442, f32[144,768]{1,0:T(8,128)S(1)} %fusion.14), kind=kOutput, calls=%fused_computation.10 | convolution fusion | flops 1133494272 | bytes 9782272 | tf_op jit(solution)/shard_map/while/body/eval_jaxpr/cond/branch_1_fun/dot_general | solution.py:46
  231.3 4.6 %all-to-all-start.1 = ((bf16[16,9,2560]{2,1,0:T(8,128)(2,1)}), bf16[16,9,2560]{2,1,0:T(8,128)(2,1)S(1)}, u32[]{:S(2)}, u32[]{:S(2)}) async-start(bf16[16,9,2560]{2,1,0:T(8,128)(2,1)} %reshape.245), calls=%async_computation.1 | async-start | bytes 2621440 | tf_op jit(solution)/shard_map/while/body/eval_jaxpr/all_to_all | solution.py:100
  240.1 26.5 %all-to-all-done.1 = bf16[16,9,2560]{2,1,0:T(8,128)(2,1)S(1)} async-done(((bf16[16,9,2560]{2,1,0:T(8,128)(2,1)}), bf16[16,9,2560]{2,1,0:T(8,128)(2,1)S(1)}, u32[]{:S(2)}, u32[]{:S(2)}) %all-to-all-start.1) | async-done | bytes 737312 | tf_op jit(solution)/shard_map/while/body/eval_jaxpr/all_to_all | solution.py:100
  276.3 4.8 %all-to-all-start = ((bf16[16,9,2560]{2,1,0:T(8,128)(2,1)}), bf16[16,9,2560]{2,1,0:T(8,128)(2,1)S(1)}, u32[]{:S(2)}, u32[]{:S(2)}) async-start(bf16[16,9,2560]{2,1,0:T(8,128)(2,1)} %reshape.244), calls=%async_computation | async-start | bytes 2621440 | tf_op jit(solution)/shard_map/while/body/eval_jaxpr/all_to_all | solution.py:93
  284.8 27.1 %all-to-all-done = bf16[16,9,2560]{2,1,0:T(8,128)(2,1)S(1)} async-done(((bf16[16,9,2560]{2,1,0:T(8,128)(2,1)}), bf16[16,9,2560]{2,1,0:T(8,128)(2,1)S(1)}, u32[]{:S(2)}, u32[]{:S(2)}) %all-to-all-start) | async-done | bytes 737312 | tf_op jit(solution)/shard_map/while/body/eval_jaxpr/all_to_all | solution.py:93
  311.9 8.3 %conditional.3 = (bf16[144,2560]{1,0:T(8,128)(2,1)S(1)}) conditional(s32[]{:T(128)} %convert_element_type.207, () %tuple.69, (bf16[2,1,1,2560,768]{4,3,2,1,0:T(8,128)(2,1)}, s32[]{:T(128)}, bf16[16,9,2560]{2,1,0:T(8,128)(2,1)S(1)}, bf16[2,1,1,2560,768]{4,3,2,1,0:T(8,128)(2,1)}, bf16[2,1,1,768,2560]{4,3,2,1,0:T(8,128)(2,1)}) %tuple.70), branch_computations={%region_8.8_spmd, %region_9.9_spmd} | conditional | flops 1699725312 | bytes 16369160 | solution.py:94
  315.1 5.1 %fusion.11 = bf16[144,2560]{1,0:T(8,128)(2,1)S(1)} fusion(bf16[2,1,1,768,2560]{4,3,2,1,0:T(8,128)(2,1)} %get-tuple-element.443, s32[]{:T(128)} %get-tuple-element.440, bf16[144,2560]{1,0:T(8,128)(2,1)S(1)} %reshape.229, bf16[2,1,1,2560,768]{4,3,2,1,0:T(8,128)(2,1)} %get-tuple-element.442, f32[144,768]{1,0:T(8,128)S(1)} %fusion.14), kind=kOutput, calls=%fused_computation.10 | convolution fusion | flops 1133494272 | bytes 9782272 | tf_op jit(solution)/shard_map/while/body/eval_jaxpr/cond/branch_1_fun/dot_general | solution.py:46
  321.6 4.6 %all-to-all-start.1 = ((bf16[16,9,2560]{2,1,0:T(8,128)(2,1)}), bf16[16,9,2560]{2,1,0:T(8,128)(2,1)S(1)}, u32[]{:S(2)}, u32[]{:S(2)}) async-start(bf16[16,9,2560]{2,1,0:T(8,128)(2,1)} %reshape.245), calls=%async_computation.1 | async-start | bytes 2621440 | tf_op jit(solution)/shard_map/while/body/eval_jaxpr/all_to_all | solution.py:100
  330.5 26.5 %all-to-all-done.1 = bf16[16,9,2560]{2,1,0:T(8,128)(2,1)S(1)} async-done(((bf16[16,9,2560]{2,1,0:T(8,128)(2,1)}), bf16[16,9,2560]{2,1,0:T(8,128)(2,1)S(1)}, u32[]{:S(2)}, u32[]{:S(2)}) %all-to-all-start.1) | async-done | bytes 737312 | tf_op jit(solution)/shard_map/while/body/eval_jaxpr/all_to_all | solution.py:100
  366.6 4.8 %all-to-all-start = ((bf16[16,9,2560]{2,1,0:T(8,128)(2,1)}), bf16[16,9,2560]{2,1,0:T(8,128)(2,1)S(1)}, u32[]{:S(2)}, u32[]{:S(2)}) async-start(bf16[16,9,2560]{2,1,0:T(8,128)(2,1)} %reshape.244), calls=%async_computation | async-start | bytes 2621440 | tf_op jit(solution)/shard_map/while/body/eval_jaxpr/all_to_all | solution.py:93
  375.1 27.1 %all-to-all-done = bf16[16,9,2560]{2,1,0:T(8,128)(2,1)S(1)} async-done(((bf16[16,9,2560]{2,1,0:T(8,128)(2,1)}), bf16[16,9,2560]{2,1,0:T(8,128)(2,1)S(1)}, u32[]{:S(2)}, u32[]{:S(2)}) %all-to-all-start) | async-done | bytes 737312 | tf_op jit(solution)/shard_map/while/body/eval_jaxpr/all_to_all | solution.py:93
  402.2 8.3 %conditional.3 = (bf16[144,2560]{1,0:T(8,128)(2,1)S(1)}) conditional(s32[]{:T(128)} %convert_element_type.207, () %tuple.69, (bf16[2,1,1,2560,768]{4,3,2,1,0:T(8,128)(2,1)}, s32[]{:T(128)}, bf16[16,9,2560]{2,1,0:T(8,128)(2,1)S(1)}, bf16[2,1,1,2560,768]{4,3,2,1,0:T(8,128)(2,1)}, bf16[2,1,1,768,2560]{4,3,2,1,0:T(8,128)(2,1)}) %tuple.70), branch_computations={%region_8.8_spmd, %region_9.9_spmd} | conditional | flops 1699725312 | bytes 16369160 | solution.py:94
  405.4 5.1 %fusion.11 = bf16[144,2560]{1,0:T(8,128)(2,1)S(1)} fusion(bf16[2,1,1,768,2560]{4,3,2,1,0:T(8,128)(2,1)} %get-tuple-element.443, s32[]{:T(128)} %get-tuple-element.440, bf16[144,2560]{1,0:T(8,128)(2,1)S(1)} %reshape.229, bf16[2,1,1,2560,768]{4,3,2,1,0:T(8,128)(2,1)} %get-tuple-element.442, f32[144,768]{1,0:T(8,128)S(1)} %fusion.14), kind=kOutput, calls=%fused_computation.10 | convolution fusion | flops 1133494272 | bytes 9782272 | tf_op jit(solution)/shard_map/while/body/eval_jaxpr/cond/branch_1_fun/dot_general | solution.py:46
  411.9 4.6 %all-to-all-start.1 = ((bf16[16,9,2560]{2,1,0:T(8,128)(2,1)}), bf16[16,9,2560]{2,1,0:T(8,128)(2,1)S(1)}, u32[]{:S(2)}, u32[]{:S(2)}) async-start(bf16[16,9,2560]{2,1,0:T(8,128)(2,1)} %reshape.245), calls=%async_computation.1 | async-start | bytes 2621440 | tf_op jit(solution)/shard_map/while/body/eval_jaxpr/all_to_all | solution.py:100
  418.4 28.9 %all-to-all-done.1 = bf16[16,9,2560]{2,1,0:T(8,128)(2,1)S(1)} async-done(((bf16[16,9,2560]{2,1,0:T(8,128)(2,1)}), bf16[16,9,2560]{2,1,0:T(8,128)(2,1)S(1)}, u32[]{:S(2)}, u32[]{:S(2)}) %all-to-all-start.1) | async-done | bytes 737312 | tf_op jit(solution)/shard_map/while/body/eval_jaxpr/all_to_all | solution.py:100
  448.1 4.4 collective-permute-done.1
  (187 shorter events, 94.1 us)
Async XLA Ops:
  5.3 37.0 %all-to-all-start = ((bf16[16,9,2560]{2,1,0:T(8,128)(2,1)}), bf16[16,9,2560]{2,1,0:T(8,128)(2,1)S(1)}, u32[]{:S(2)}, u32[]{:S(2)}) async-start(bf16[16,9,2560]{2,1,0:T(8,128)(2,1)} %reshape.244), calls=%async_computation | async-start | bytes 2621440 | tf_op jit(solution)/shard_map/while/body/eval_jaxpr/all_to_all | solution.py:93
  11.4 77.2 %collective-permute-start.2 = (bf16[16,2560]{1,0:T(8,128)(2,1)S(1)}, bf16[16,2560]{1,0:T(8,128)(2,1)S(1)}, u32[]{:S(2)}, u32[]{:S(2)}) collective-permute-start(bf16[16,2560]{1,0:T(8,128)(2,1)S(1)} %copy.43), channel_id=1, source_target_pairs={{16,0},{17,1},{18,2},{19,3},{20,4},{21,5},{22,6},{23,7},{24,8},{25... | collective-permute-start | bytes 245768 | tf_op jit(solution)/shard_map/while/body/eval_jaxpr/ppermute | solution.py:15
  42.3 16.7 %copy-start.1 = (bf16[2,1,2560,16]{2,3,1,0:T(8,128)(2,1)S(1)}, bf16[2,1,2560,16]{2,3,1,0:T(8,128)(2,1)}, u32[]{:S(2)}) copy-start(bf16[2,1,2560,16]{2,3,1,0:T(8,128)(2,1)} %get-tuple-element.725) | copy-start | bytes 491524 | tf_op jit(solution)/shard_map/while
  43.7 35.4 %all-to-all-start.1 = ((bf16[16,9,2560]{2,1,0:T(8,128)(2,1)}), bf16[16,9,2560]{2,1,0:T(8,128)(2,1)S(1)}, u32[]{:S(2)}, u32[]{:S(2)}) async-start(bf16[16,9,2560]{2,1,0:T(8,128)(2,1)} %reshape.245), calls=%async_computation.1 | async-start | bytes 2621440 | tf_op jit(solution)/shard_map/while/body/eval_jaxpr/all_to_all | solution.py:100
  48.3 31.3 %collective-permute-start = (bf16[16,2560]{1,0:T(8,128)(2,1)S(1)}, bf16[16,2560]{1,0:T(8,128)(2,1)S(1)}, u32[]{:S(2)}, u32[]{:S(2)}) collective-permute-start(bf16[16,2560]{1,0:T(8,128)(2,1)S(1)} %broadcast_select_fusion.6), channel_id=1, source_target_pairs={{16,0},{17,1},{18,2},{19,3},{20,4},{21,5},{22,6},{23,7},{24,8},{25... | collective-permute-start | bytes 245768 | tf_op jit(solution)/shard_map/while/body/eval_jaxpr/ppermute | solution.py:15
  79.8 11.2 %collective-permute-start.1 = (bf16[16,2560]{1,0:T(8,128)(2,1)S(1)}, bf16[16,2560]{1,0:T(8,128)(2,1)S(1)}, u32[]{:S(2)}, u32[]{:S(2)}) collective-permute-start(bf16[16,2560]{1,0:T(8,128)(2,1)S(1)} %get-tuple-element.674), channel_id=1, source_target_pairs={{0,16},{16,0},{1,17},{17,1},{2,18},{18,2},{3,19},{19,3},{4,20},{20... | collective-permute-start | bytes 245768 | tf_op jit(solution)/shard_map/while/body/eval_jaxpr/ppermute | solution.py:9
  95.4 35.9 %all-to-all-start = ((bf16[16,9,2560]{2,1,0:T(8,128)(2,1)}), bf16[16,9,2560]{2,1,0:T(8,128)(2,1)S(1)}, u32[]{:S(2)}, u32[]{:S(2)}) async-start(bf16[16,9,2560]{2,1,0:T(8,128)(2,1)} %reshape.244), calls=%async_computation | async-start | bytes 2621440 | tf_op jit(solution)/shard_map/while/body/eval_jaxpr/all_to_all | solution.py:93
  100.5 78.5 %collective-permute-start.2 = (bf16[16,2560]{1,0:T(8,128)(2,1)S(1)}, bf16[16,2560]{1,0:T(8,128)(2,1)S(1)}, u32[]{:S(2)}, u32[]{:S(2)}) collective-permute-start(bf16[16,2560]{1,0:T(8,128)(2,1)S(1)} %copy.43), channel_id=1, source_target_pairs={{16,0},{17,1},{18,2},{19,3},{20,4},{21,5},{22,6},{23,7},{24,8},{25... | collective-permute-start | bytes 245768 | tf_op jit(solution)/shard_map/while/body/eval_jaxpr/ppermute | solution.py:15
  139.6 9.7 %copy-start.1 = (bf16[2,1,2560,16]{2,3,1,0:T(8,128)(2,1)S(1)}, bf16[2,1,2560,16]{2,3,1,0:T(8,128)(2,1)}, u32[]{:S(2)}) copy-start(bf16[2,1,2560,16]{2,3,1,0:T(8,128)(2,1)} %get-tuple-element.725) | copy-start | bytes 491524 | tf_op jit(solution)/shard_map/while
  140.9 35.4 %all-to-all-start.1 = ((bf16[16,9,2560]{2,1,0:T(8,128)(2,1)}), bf16[16,9,2560]{2,1,0:T(8,128)(2,1)S(1)}, u32[]{:S(2)}, u32[]{:S(2)}) async-start(bf16[16,9,2560]{2,1,0:T(8,128)(2,1)} %reshape.245), calls=%async_computation.1 | async-start | bytes 2621440 | tf_op jit(solution)/shard_map/while/body/eval_jaxpr/all_to_all | solution.py:100
  145.6 31.3 %collective-permute-start = (bf16[16,2560]{1,0:T(8,128)(2,1)S(1)}, bf16[16,2560]{1,0:T(8,128)(2,1)S(1)}, u32[]{:S(2)}, u32[]{:S(2)}) collective-permute-start(bf16[16,2560]{1,0:T(8,128)(2,1)S(1)} %broadcast_select_fusion.6), channel_id=1, source_target_pairs={{16,0},{17,1},{18,2},{19,3},{20,4},{21,5},{22,6},{23,7},{24,8},{25... | collective-permute-start | bytes 245768 | tf_op jit(solution)/shard_map/while/body/eval_jaxpr/ppermute | solution.py:15
  177.1 4.5 collective-permute-start.1
  186.0 35.6 %all-to-all-start = ((bf16[16,9,2560]{2,1,0:T(8,128)(2,1)}), bf16[16,9,2560]{2,1,0:T(8,128)(2,1)S(1)}, u32[]{:S(2)}, u32[]{:S(2)}) async-start(bf16[16,9,2560]{2,1,0:T(8,128)(2,1)} %reshape.244), calls=%async_computation | async-start | bytes 2621440 | tf_op jit(solution)/shard_map/while/body/eval_jaxpr/all_to_all | solution.py:93
  190.8 78.5 %collective-permute-start.2 = (bf16[16,2560]{1,0:T(8,128)(2,1)S(1)}, bf16[16,2560]{1,0:T(8,128)(2,1)S(1)}, u32[]{:S(2)}, u32[]{:S(2)}) collective-permute-start(bf16[16,2560]{1,0:T(8,128)(2,1)S(1)} %copy.43), channel_id=1, source_target_pairs={{16,0},{17,1},{18,2},{19,3},{20,4},{21,5},{22,6},{23,7},{24,8},{25... | collective-permute-start | bytes 245768 | tf_op jit(solution)/shard_map/while/body/eval_jaxpr/ppermute | solution.py:15
  229.9 9.7 %copy-start.1 = (bf16[2,1,2560,16]{2,3,1,0:T(8,128)(2,1)S(1)}, bf16[2,1,2560,16]{2,3,1,0:T(8,128)(2,1)}, u32[]{:S(2)}) copy-start(bf16[2,1,2560,16]{2,3,1,0:T(8,128)(2,1)} %get-tuple-element.725) | copy-start | bytes 491524 | tf_op jit(solution)/shard_map/while
  231.3 35.4 %all-to-all-start.1 = ((bf16[16,9,2560]{2,1,0:T(8,128)(2,1)}), bf16[16,9,2560]{2,1,0:T(8,128)(2,1)S(1)}, u32[]{:S(2)}, u32[]{:S(2)}) async-start(bf16[16,9,2560]{2,1,0:T(8,128)(2,1)} %reshape.245), calls=%async_computation.1 | async-start | bytes 2621440 | tf_op jit(solution)/shard_map/while/body/eval_jaxpr/all_to_all | solution.py:100
  235.9 31.3 %collective-permute-start = (bf16[16,2560]{1,0:T(8,128)(2,1)S(1)}, bf16[16,2560]{1,0:T(8,128)(2,1)S(1)}, u32[]{:S(2)}, u32[]{:S(2)}) collective-permute-start(bf16[16,2560]{1,0:T(8,128)(2,1)S(1)} %broadcast_select_fusion.6), channel_id=1, source_target_pairs={{16,0},{17,1},{18,2},{19,3},{20,4},{21,5},{22,6},{23,7},{24,8},{25... | collective-permute-start | bytes 245768 | tf_op jit(solution)/shard_map/while/body/eval_jaxpr/ppermute | solution.py:15
  267.4 4.5 collective-permute-start.1
  276.3 35.6 %all-to-all-start = ((bf16[16,9,2560]{2,1,0:T(8,128)(2,1)}), bf16[16,9,2560]{2,1,0:T(8,128)(2,1)S(1)}, u32[]{:S(2)}, u32[]{:S(2)}) async-start(bf16[16,9,2560]{2,1,0:T(8,128)(2,1)} %reshape.244), calls=%async_computation | async-start | bytes 2621440 | tf_op jit(solution)/shard_map/while/body/eval_jaxpr/all_to_all | solution.py:93
  281.1 78.5 %collective-permute-start.2 = (bf16[16,2560]{1,0:T(8,128)(2,1)S(1)}, bf16[16,2560]{1,0:T(8,128)(2,1)S(1)}, u32[]{:S(2)}, u32[]{:S(2)}) collective-permute-start(bf16[16,2560]{1,0:T(8,128)(2,1)S(1)} %copy.43), channel_id=1, source_target_pairs={{16,0},{17,1},{18,2},{19,3},{20,4},{21,5},{22,6},{23,7},{24,8},{25... | collective-permute-start | bytes 245768 | tf_op jit(solution)/shard_map/while/body/eval_jaxpr/ppermute | solution.py:15
  320.2 9.7 %copy-start.1 = (bf16[2,1,2560,16]{2,3,1,0:T(8,128)(2,1)S(1)}, bf16[2,1,2560,16]{2,3,1,0:T(8,128)(2,1)}, u32[]{:S(2)}) copy-start(bf16[2,1,2560,16]{2,3,1,0:T(8,128)(2,1)} %get-tuple-element.725) | copy-start | bytes 491524 | tf_op jit(solution)/shard_map/while
  321.6 35.4 %all-to-all-start.1 = ((bf16[16,9,2560]{2,1,0:T(8,128)(2,1)}), bf16[16,9,2560]{2,1,0:T(8,128)(2,1)S(1)}, u32[]{:S(2)}, u32[]{:S(2)}) async-start(bf16[16,9,2560]{2,1,0:T(8,128)(2,1)} %reshape.245), calls=%async_computation.1 | async-start | bytes 2621440 | tf_op jit(solution)/shard_map/while/body/eval_jaxpr/all_to_all | solution.py:100
  326.2 31.3 %collective-permute-start = (bf16[16,2560]{1,0:T(8,128)(2,1)S(1)}, bf16[16,2560]{1,0:T(8,128)(2,1)S(1)}, u32[]{:S(2)}, u32[]{:S(2)}) collective-permute-start(bf16[16,2560]{1,0:T(8,128)(2,1)S(1)} %broadcast_select_fusion.6), channel_id=1, source_target_pairs={{16,0},{17,1},{18,2},{19,3},{20,4},{21,5},{22,6},{23,7},{24,8},{25... | collective-permute-start | bytes 245768 | tf_op jit(solution)/shard_map/while/body/eval_jaxpr/ppermute | solution.py:15
  357.7 4.5 collective-permute-start.1
  366.6 35.6 %all-to-all-start = ((bf16[16,9,2560]{2,1,0:T(8,128)(2,1)}), bf16[16,9,2560]{2,1,0:T(8,128)(2,1)S(1)}, u32[]{:S(2)}, u32[]{:S(2)}) async-start(bf16[16,9,2560]{2,1,0:T(8,128)(2,1)} %reshape.244), calls=%async_computation | async-start | bytes 2621440 | tf_op jit(solution)/shard_map/while/body/eval_jaxpr/all_to_all | solution.py:93
  371.4 76.7 %collective-permute-start.2 = (bf16[16,2560]{1,0:T(8,128)(2,1)S(1)}, bf16[16,2560]{1,0:T(8,128)(2,1)S(1)}, u32[]{:S(2)}, u32[]{:S(2)}) collective-permute-start(bf16[16,2560]{1,0:T(8,128)(2,1)S(1)} %copy.43), channel_id=1, source_target_pairs={{16,0},{17,1},{18,2},{19,3},{20,4},{21,5},{22,6},{23,7},{24,8},{25... | collective-permute-start | bytes 245768 | tf_op jit(solution)/shard_map/while/body/eval_jaxpr/ppermute | solution.py:15
  410.5 7.3 %copy-start.1 = (bf16[2,1,2560,16]{2,3,1,0:T(8,128)(2,1)S(1)}, bf16[2,1,2560,16]{2,3,1,0:T(8,128)(2,1)}, u32[]{:S(2)}) copy-start(bf16[2,1,2560,16]{2,3,1,0:T(8,128)(2,1)} %get-tuple-element.725) | copy-start | bytes 491524 | tf_op jit(solution)/shard_map/while
  411.9 35.4 %all-to-all-start.1 = ((bf16[16,9,2560]{2,1,0:T(8,128)(2,1)}), bf16[16,9,2560]{2,1,0:T(8,128)(2,1)S(1)}, u32[]{:S(2)}, u32[]{:S(2)}) async-start(bf16[16,9,2560]{2,1,0:T(8,128)(2,1)} %reshape.245), calls=%async_computation.1 | async-start | bytes 2621440 | tf_op jit(solution)/shard_map/while/body/eval_jaxpr/all_to_all | solution.py:100
  416.5 31.3 %collective-permute-start = (bf16[16,2560]{1,0:T(8,128)(2,1)S(1)}, bf16[16,2560]{1,0:T(8,128)(2,1)S(1)}, u32[]{:S(2)}, u32[]{:S(2)}) collective-permute-start(bf16[16,2560]{1,0:T(8,128)(2,1)S(1)} %broadcast_select_fusion.6), channel_id=1, source_target_pairs={{16,0},{17,1},{18,2},{19,3},{20,4},{21,5},{22,6},{23,7},{24,8},{25... | collective-permute-start | bytes 245768 | tf_op jit(solution)/shard_map/while/body/eval_jaxpr/ppermute | solution.py:15
  448.1 4.5 collective-permute-start.1
  452.6 0.6 copy-start
where the time goes:
time: 455 us; the launch traced here: 453 us
  waiting for transfers between devices  280 us (62%)
  starting transfers between devices  103 us (23%)
  matrix products  37 us (8%)
  local copies, waits for them, and re-layouts  27.4 us (6%)
  other arithmetic  4.87 us (1%)
    all_to_all x5, waiting for transfers between devices, layer(): lax.all_to_all(sending, 'expert', split_axis=0, concat_axis=0, tiled=True)  137 us
    all_to_all x5, waiting for transfers between devices, layer(): lax.all_to_all(answered, 'expert', split_axis=0, concat_axis=0, tiled=True)  128 us
    ppermute x10, starting transfers between devices, passed_along_2(): return lax.ppermute(block, axis, route)  39.8 us
    all_to_all x5, starting transfers between devices, layer(): lax.all_to_all(sending, 'expert', split_axis=0, concat_axis=0, tiled=True)  25.8 us
    all_to_all x5, starting transfers between devices, layer(): lax.all_to_all(answered, 'expert', split_axis=0, concat_axis=0, tiled=True)  23.2 us
    dot_general x4, matrix products, expert_rows(): jnp.dot(hidden, down_mat, preferred_element_type=jnp.float32)  20.4 us
    ppermute x5, waiting for transfers between devices, passed_along(): lax.ppermute(array, axis, [(i, (i + by) % size) for i in range(size)])  14.9 us
    ppermute x5, starting transfers between devices, passed_along(): lax.ppermute(array, axis, [(i, (i + by) % size) for i in range(size)])  14.3 us
  transfers between devices with their start and end apart: 25, of which 15 were waited for; matrix products, arithmetic and copies ran while one was open for 10% of the time, Pallas kernels for 0%

commit v1 on v0

--- a/solution.py
+++ b/solution.py
@@ -2,6 +2,18 @@
 import jax.numpy as jnp
 from jax import lax
 from jax.sharding import PartitionSpec as P
+
+
+def split_up(x, dim, devices):
+    dims = x.shape
+    tiles = x.reshape(*dims[:dim], devices, dims[dim] // devices, *dims[dim + 1 :])
+    return jnp.moveaxis(tiles, dim, 0)
+
+
+def in_order(blocks, dim):
+    blocks = jnp.moveaxis(blocks, 0, dim)
+    dims = blocks.shape
+    return blocks.reshape(*dims[:dim], dims[dim] * dims[dim + 1], *dims[dim + 2 :])
 
 
 def passed_along(array, axis, by):
@@ -97,7 +109,16 @@
             jnp.zeros_like,
             received.reshape(-1, feature),
         ).reshape(received.shape)
-        returned = lax.all_to_all(answered, "expert", split_axis=0, concat_axis=0, tiled=True)
+        size_2, index = (lax.axis_size("expert"), lax.axis_index("expert"))
+        blocks_2 = split_up(answered, 0, size_2)
+        finished = [blocks_2[index]]
+        for lap in range(1, size_2):
+            sent = blocks_2[index ^ lap]
+            finished.append(
+                lax.ppermute(sent, "expert", [(i_2, i_2 ^ lap) for i_2 in range(size_2)])
+            )
+        blocks_2 = jnp.stack(finished)[index ^ jnp.arange(size_2)]
+        returned = in_order(blocks_2, 0)
         mixed = weighted_rows(combine, returned.reshape(-1, feature))
         return ((slab_in.astype(jnp.float32) + mixed).astype(jnp.bfloat16), micro_at)
 

time: 455 us -> 506 us (1.11)
  starting transfers between devices: 103 us -> 135 us
  local copies, waits for them, and re-layouts: 27.4 us -> 35 us
    all_to_all x5 -> x0, waiting for transfers between devices: 128 us -> none  [layer(): lax.all_to_all(answered, 'expert', split_axis=0, concat_axis=0, tiled=True)]
    ppermute x0 -> x75, waiting for transfers between devices: none -> 126 us  [layer(): lax.ppermute(sent, 'expert', [(i_2, i_2 ^ lap) for i_2 in range(size_2)])]
    ppermute x0 -> x75, starting transfers between devices: none -> 75.8 us  [layer(): lax.ppermute(sent, 'expert', [(i_2, i_2 ^ lap) for i_2 in range(size_2)])]
    all_to_all x5 -> x0, starting transfers between devices: 23.2 us -> none  [layer(): lax.all_to_all(answered, 'expert', split_axis=0, concat_axis=0, tiled=True)]
    ppermute x10, starting transfers between devices: 39.8 us -> 25.3 us  [passed_along_2(): return lax.ppermute(block, axis, route)]
    ppermute x5, starting transfers between devices: 14.3 us -> 7.62 us  [passed_along(): lax.ppermute(array, axis, [(i, (i + by) % size) for i in range(size)])]
    ppermute x5, waiting for transfers between devices: 14.9 us -> 20.5 us  [passed_along(): lax.ppermute(array, axis, [(i, (i + by) % size) for i in range(size)])]
    reshape x5, local copies, waits for them, and re-layouts: 6.79 us -> 1.3 us  [split_up(): x.reshape(*dims[:dim], devices, dims[dim] // devices, *dims[dim + 1:])]
  transfers between devices with their start and end apart: 25 -> 95, of which waited for: 15 -> 70; matrix products, arithmetic and copies ran while one was open for 10% -> 15% of each run, Pallas kernels for 0% -> 0%
where the time goes in v1:
time: 506 us; the launch traced here: 504 us
  waiting for transfers between devices  285 us (56%)
  starting transfers between devices  135 us (27%)
  matrix products  39.7 us (8%)
  local copies, waits for them, and re-layouts  35 us (7%)
  other arithmetic  8.13 us (2%)
    all_to_all x5, waiting for transfers between devices, layer(): lax.all_to_all(sending, 'expert', split_axis=0, concat_axis=0, tiled=True)  138 us
    ppermute x75, waiting for transfers between devices, layer(): lax.ppermute(sent, 'expert', [(i_2, i_2 ^ lap) for i_2 in range(size_2)])  126 us
    ppermute x75, starting transfers between devices, layer(): lax.ppermute(sent, 'expert', [(i_2, i_2 ^ lap) for i_2 in range(size_2)])  75.8 us
    all_to_all x5, starting transfers between devices, layer(): lax.all_to_all(sending, 'expert', split_axis=0, concat_axis=0, tiled=True)  26.3 us
    ppermute x10, starting transfers between devices, passed_along_2(): return lax.ppermute(block, axis, route)  25.3 us
    ppermute x5, waiting for transfers between devices, passed_along(): lax.ppermute(array, axis, [(i, (i + by) % size) for i in range(size)])  20.5 us
    dot_general x4, matrix products, expert_rows(): jnp.dot(hidden, down_mat, preferred_element_type=jnp.float32)  20.4 us
    dot_general x4, matrix products, expert_rows(): gate_proj = jnp.dot(rows_in, gate_mat, preferred_element_type=jnp.float32)  11.4 us
  transfers between devices with their start and end apart: 95, of which 70 were waited for; matrix products, arithmetic and copies ran while one was open for 15% of the time, Pallas kernels for 0%

profile of v1, /device:TPU:20, one launch (start us, length us, event | category | flops | bytes accessed | tf_op | source)
XLA Modules:
  0.0 503.7 jit_solution(9480127422657687404)
XLA Ops:
  1.5 501.5 %while.21 = (s32[]{:T(128)}, bf16[16,2560]{1,0:T(8,128)(2,1)S(1)}, bf16[16,2560]{1,0:T(8,128)(2,1)}, bf16[16,2560]{1,0:T(8,128)(2,1)S(1)}, pred[]{:T(512)}, /*in...) while((s32[]{:T(128)}, bf16[16,2560]{1,0:T(8,128)(2,1)S(1)}, ...), condition=%wide.region_10.11_spmd.clone, body=%wide.region_0.10_spmd.clone.sunk | while | flops 1737770624 | bytes 38125556 | solution.py:140
  9.8 6.3 %all-to-all-start = ((bf16[16,9,2560]{2,1,0:T(8,128)(2,1)}), bf16[16,9,2560]{2,1,0:T(8,128)(2,1)S(1)}, u32[]{:S(2)}, u32[]{:S(2)}) async-start(bf16[16,9,2560]{2,1,0:T(8,128)(2,1)} %reshape.280), calls=%async_computation | async-start | bytes 2621440 | tf_op jit(solution)/shard_map/while/body/eval_jaxpr/all_to_all | solution.py:105
  19.2 27.7 %all-to-all-done = bf16[16,9,2560]{2,1,0:T(8,128)(2,1)S(1)} async-done(((bf16[16,9,2560]{2,1,0:T(8,128)(2,1)}), bf16[16,9,2560]{2,1,0:T(8,128)(2,1)S(1)}, u32[]{:S(2)}, u32[]{:S(2)}) %all-to-all-start) | async-done | bytes 737312 | tf_op jit(solution)/shard_map/while/body/eval_jaxpr/all_to_all | solution.py:105
  80.8 3.9 collective-permute-done.13
  90.7 7.3 %collective-permute-start.16 = (bf16[16,2560]{1,0:T(8,128)(2,1)S(1)}, bf16[16,2560]{1,0:T(8,128)(2,1)S(1)}, u32[]{:S(2)}, u32[]{:S(2)}) collective-permute-start(bf16[16,2560]{1,0:T(8,128)(2,1)S(1)} %get-tuple-element.723), channel_id=1, source_target_pairs={{0,16},{16,0},{1,17},{17,1},{2,18},{18,2},{3,19},{19,3},{4,20},{20... | collective-permute-start | bytes 245768 | tf_op jit(solution)/shard_map/while/body/eval_jaxpr/ppermute | solution.py:21
  101.6 4.3 collective-permute-start.17
  110.2 5.0 all-to-all-start
  118.4 27.7 %all-to-all-done = bf16[16,9,2560]{2,1,0:T(8,128)(2,1)S(1)} async-done(((bf16[16,9,2560]{2,1,0:T(8,128)(2,1)}), bf16[16,9,2560]{2,1,0:T(8,128)(2,1)S(1)}, u32[]{:S(2)}, u32[]{:S(2)}) %all-to-all-start) | async-done | bytes 737312 | tf_op jit(solution)/shard_map/while/body/eval_jaxpr/all_to_all | solution.py:105
  146.0 8.6 %conditional.3 = (bf16[16,1,9,2560]{3,2,0,1:T(8,128)(2,1)S(1)}) conditional(s32[]{:T(128)} %convert_element_type.207, () %tuple.88, (bf16[2,1,1,2560,768]{4,3,2,1,0:T(8,128)(2,1)}, s32[]{:T(128)}, bf16[16,9,2560]{2,1,0:T(8,128)(2,1)S(1)}, bf16[2,1,1,2560,768]{4,3,2,1,0:T(8,128)(2,1)}, bf16[2,1,1,768,2560]{4,3,2,1,0:T(8,128)(2,1)}) %tuple.89), branch_computations={%region_8.8_spmd, %region_9.9_spmd} | conditional | flops 1699725312 | bytes 17843720 | solution.py:106
  149.2 5.1 %fusion.11 = bf16[144,2560]{1,0:T(8,128)(2,1)S(1)} fusion(bf16[2,1,1,768,2560]{4,3,2,1,0:T(8,128)(2,1)} %get-tuple-element.444, s32[]{:T(128)} %get-tuple-element.441, bf16[144,2560]{1,0:T(8,128)(2,1)S(1)} %reshape.248, bf16[2,1,1,2560,768]{4,3,2,1,0:T(8,128)(2,1)} %get-tuple-element.443, f32[144,768]{1,0:T(8,128)S(1)} %fusion.14), kind=kOutput, calls=%fused_computation.11 | convolution fusion | flops 1133494272 | bytes 9782272 | tf_op jit(solution)/shard_map/while/body/eval_jaxpr/cond/branch_1_fun/dot_general | solution.py:58
  157.4 3.6 collective-permute-done.2
  188.4 3.9 collective-permute-done.13
  198.4 4.4 collective-permute-done.16
  210.9 5.0 all-to-all-start
  219.0 27.7 %all-to-all-done = bf16[16,9,2560]{2,1,0:T(8,128)(2,1)S(1)} async-done(((bf16[16,9,2560]{2,1,0:T(8,128)(2,1)}), bf16[16,9,2560]{2,1,0:T(8,128)(2,1)S(1)}, u32[]{:S(2)}, u32[]{:S(2)}) %all-to-all-start) | async-done | bytes 737312 | tf_op jit(solution)/shard_map/while/body/eval_jaxpr/all_to_all | solution.py:105
  246.7 8.6 %conditional.3 = (bf16[16,1,9,2560]{3,2,0,1:T(8,128)(2,1)S(1)}) conditional(s32[]{:T(128)} %convert_element_type.207, () %tuple.88, (bf16[2,1,1,2560,768]{4,3,2,1,0:T(8,128)(2,1)}, s32[]{:T(128)}, bf16[16,9,2560]{2,1,0:T(8,128)(2,1)S(1)}, bf16[2,1,1,2560,768]{4,3,2,1,0:T(8,128)(2,1)}, bf16[2,1,1,768,2560]{4,3,2,1,0:T(8,128)(2,1)}) %tuple.89), branch_computations={%region_8.8_spmd, %region_9.9_spmd} | conditional | flops 1699725312 | bytes 17843720 | solution.py:106
  249.9 5.1 %fusion.11 = bf16[144,2560]{1,0:T(8,128)(2,1)S(1)} fusion(bf16[2,1,1,768,2560]{4,3,2,1,0:T(8,128)(2,1)} %get-tuple-element.444, s32[]{:T(128)} %get-tuple-element.441, bf16[144,2560]{1,0:T(8,128)(2,1)S(1)} %reshape.248, bf16[2,1,1,2560,768]{4,3,2,1,0:T(8,128)(2,1)} %get-tuple-element.443, f32[144,768]{1,0:T(8,128)S(1)} %fusion.14), kind=kOutput, calls=%fused_computation.11 | convolution fusion | flops 1133494272 | bytes 9782272 | tf_op jit(solution)/shard_map/while/body/eval_jaxpr/cond/branch_1_fun/dot_general | solution.py:58
  258.1 3.6 collective-permute-done.2
  289.1 3.9 collective-permute-done.13
  299.1 4.5 collective-permute-done.16
  311.5 5.0 all-to-all-start
  319.7 27.7 %all-to-all-done = bf16[16,9,2560]{2,1,0:T(8,128)(2,1)S(1)} async-done(((bf16[16,9,2560]{2,1,0:T(8,128)(2,1)}), bf16[16,9,2560]{2,1,0:T(8,128)(2,1)S(1)}, u32[]{:S(2)}, u32[]{:S(2)}) %all-to-all-start) | async-done | bytes 737312 | tf_op jit(solution)/shard_map/while/body/eval_jaxpr/all_to_all | solution.py:105
  347.4 8.6 %conditional.3 = (bf16[16,1,9,2560]{3,2,0,1:T(8,128)(2,1)S(1)}) conditional(s32[]{:T(128)} %convert_element_type.207, () %tuple.88, (bf16[2,1,1,2560,768]{4,3,2,1,0:T(8,128)(2,1)}, s32[]{:T(128)}, bf16[16,9,2560]{2,1,0:T(8,128)(2,1)S(1)}, bf16[2,1,1,2560,768]{4,3,2,1,0:T(8,128)(2,1)}, bf16[2,1,1,768,2560]{4,3,2,1,0:T(8,128)(2,1)}) %tuple.89), branch_computations={%region_8.8_spmd, %region_9.9_spmd} | conditional | flops 1699725312 | bytes 17843720 | solution.py:106
  350.5 5.1 %fusion.11 = bf16[144,2560]{1,0:T(8,128)(2,1)S(1)} fusion(bf16[2,1,1,768,2560]{4,3,2,1,0:T(8,128)(2,1)} %get-tuple-element.444, s32[]{:T(128)} %get-tuple-element.441, bf16[144,2560]{1,0:T(8,128)(2,1)S(1)} %reshape.248, bf16[2,1,1,2560,768]{4,3,2,1,0:T(8,128)(2,1)} %get-tuple-element.443, f32[144,768]{1,0:T(8,128)S(1)} %fusion.14), kind=kOutput, calls=%fused_computation.11 | convolution fusion | flops 1133494272 | bytes 9782272 | tf_op jit(solution)/shard_map/while/body/eval_jaxpr/cond/branch_1_fun/dot_general | solution.py:58
  389.7 3.9 collective-permute-done.13
  398.8 4.5 collective-permute-done.16
  411.3 5.0 all-to-all-start
  419.5 27.7 %all-to-all-done = bf16[16,9,2560]{2,1,0:T(8,128)(2,1)S(1)} async-done(((bf16[16,9,2560]{2,1,0:T(8,128)(2,1)}), bf16[16,9,2560]{2,1,0:T(8,128)(2,1)S(1)}, u32[]{:S(2)}, u32[]{:S(2)}) %all-to-all-start) | async-done | bytes 737312 | tf_op jit(solution)/shard_map/while/body/eval_jaxpr/all_to_all | solution.py:105
  447.1 8.6 %conditional.3 = (bf16[16,1,9,2560]{3,2,0,1:T(8,128)(2,1)S(1)}) conditional(s32[]{:T(128)} %convert_element_type.207, () %tuple.88, (bf16[2,1,1,2560,768]{4,3,2,1,0:T(8,128)(2,1)}, s32[]{:T(128)}, bf16[16,9,2560]{2,1,0:T(8,128)(2,1)S(1)}, bf16[2,1,1,2560,768]{4,3,2,1,0:T(8,128)(2,1)}, bf16[2,1,1,768,2560]{4,3,2,1,0:T(8,128)(2,1)}) %tuple.89), branch_computations={%region_8.8_spmd, %region_9.9_spmd} | conditional | flops 1699725312 | bytes 17843720 | solution.py:106
  450.3 5.1 %fusion.11 = bf16[144,2560]{1,0:T(8,128)(2,1)S(1)} fusion(bf16[2,1,1,768,2560]{4,3,2,1,0:T(8,128)(2,1)} %get-tuple-element.444, s32[]{:T(128)} %get-tuple-element.441, bf16[144,2560]{1,0:T(8,128)(2,1)S(1)} %reshape.248, bf16[2,1,1,2560,768]{4,3,2,1,0:T(8,128)(2,1)} %get-tuple-element.443, f32[144,768]{1,0:T(8,128)S(1)} %fusion.14), kind=kOutput, calls=%fused_computation.11 | convolution fusion | flops 1133494272 | bytes 9782272 | tf_op jit(solution)/shard_map/while/body/eval_jaxpr/cond/branch_1_fun/dot_general | solution.py:58
  489.5 3.9 collective-permute-done.13
  498.6 4.5 collective-permute-done.16
  (421 shorter events, 261.5 us)
Async XLA Ops:
  2.4 95.6 %collective-permute-start.17 = (bf16[16,2560]{1,0:T(8,128)(2,1)S(1)}, bf16[16,2560]{1,0:T(8,128)(2,1)}, u32[]{:S(2)}, u32[]{:S(2)}) collective-permute-start(bf16[16,2560]{1,0:T(8,128)(2,1)S(1)} %copy.58), channel_id=1, source_target_pairs={{16,0},{17,1},{18,2},{19,3},{20,4},{21,5},{22,6},{23,7},{24,8},{25... | collective-permute-start | bytes 245768 | tf_op jit(solution)/shard_map/while/body/eval_jaxpr/ppermute | solution.py:27
  9.8 37.1 %all-to-all-start = ((bf16[16,9,2560]{2,1,0:T(8,128)(2,1)}), bf16[16,9,2560]{2,1,0:T(8,128)(2,1)S(1)}, u32[]{:S(2)}, u32[]{:S(2)}) async-start(bf16[16,9,2560]{2,1,0:T(8,128)(2,1)} %reshape.280), calls=%async_computation | async-start | bytes 2621440 | tf_op jit(solution)/shard_map/while/body/eval_jaxpr/all_to_all | solution.py:105
  16.7 72.9 %collective-permute-start = (bf16[16,2560]{1,0:T(8,128)(2,1)}, bf16[16,2560]{1,0:T(8,128)(2,1)}, u32[]{:S(2)}, u32[]{:S(2)}) collective-permute-start(bf16[16,2560]{1,0:T(8,128)(2,1)} %broadcast_select_fusion.6), channel_id=1, source_target_pairs={{16,0},{17,1},{18,2},{19,3},{20,4},{21,5},{22,6},{23,7},{24,8},{25... | collective-permute-start | bytes 245768 | tf_op jit(solution)/shard_map/while/body/eval_jaxpr/ppermute | solution.py:27
  67.3 12.3 %collective-permute-start.12 = (bf16[1,9,2560]{2,1,0:T(8,128)(2,1)S(1)}, bf16[1,9,2560]{2,1,0:T(8,128)(2,1)S(1)}, u32[]{:S(2)}, u32[]{:S(2)}) collective-permute-start(bf16[1,9,2560]{2,1,0:T(8,128)(2,1)S(1)} %get-tuple-element.719), channel_id=1, source_target_pairs={{0,12},{1,13},{2,14},{3,15},{4,8},{5,9},{6,10},{7,11},{8,4},{9,5},... | collective-permute-start | bytes 138248 | tf_op jit(solution)/shard_map/while/body/eval_jaxpr/ppermute | solution.py:118
  70.9 13.8 %collective-permute-start.13 = (bf16[1,9,2560]{2,1,0:T(8,128)(2,1)S(1)}, bf16[1,9,2560]{2,1,0:T(8,128)(2,1)S(1)}, u32[]{:S(2)}, u32[]{:S(2)}) collective-permute-start(bf16[1,9,2560]{2,1,0:T(8,128)(2,1)S(1)} %get-tuple-element.720), channel_id=1, source_target_pairs={{0,13},{1,12},{2,15},{3,14},{4,9},{5,8},{6,11},{7,10},{8,5},{9,4},... | collective-permute-start | bytes 138248 | tf_op jit(solution)/shard_map/while/body/eval_jaxpr/ppermute | solution.py:118
  74.1 13.2 %collective-permute-start.14 = (bf16[1,9,2560]{2,1,0:T(8,128)(2,1)S(1)}, bf16[1,9,2560]{2,1,0:T(8,128)(2,1)S(1)}, u32[]{:S(2)}, u32[]{:S(2)}) collective-permute-start(bf16[1,9,2560]{2,1,0:T(8,128)(2,1)S(1)} %get-tuple-element.721), channel_id=1, source_target_pairs={{0,14},{1,15},{2,12},{3,13},{4,10},{5,11},{6,8},{7,9},{8,6},{9,7},... | collective-permute-start | bytes 138248 | tf_op jit(solution)/shard_map/while/body/eval_jaxpr/ppermute | solution.py:118
  90.7 10.1 %collective-permute-start.16 = (bf16[16,2560]{1,0:T(8,128)(2,1)S(1)}, bf16[16,2560]{1,0:T(8,128)(2,1)S(1)}, u32[]{:S(2)}, u32[]{:S(2)}) collective-permute-start(bf16[16,2560]{1,0:T(8,128)(2,1)S(1)} %get-tuple-element.723), channel_id=1, source_target_pairs={{0,16},{16,0},{1,17},{17,1},{2,18},{18,2},{3,19},{19,3},{4,20},{20... | collective-permute-start | bytes 245768 | tf_op jit(solution)/shard_map/while/body/eval_jaxpr/ppermute | solution.py:21
  101.6 96.8 %collective-permute-start.17 = (bf16[16,2560]{1,0:T(8,128)(2,1)S(1)}, bf16[16,2560]{1,0:T(8,128)(2,1)}, u32[]{:S(2)}, u32[]{:S(2)}) collective-permute-start(bf16[16,2560]{1,0:T(8,128)(2,1)S(1)} %copy.58), channel_id=1, source_target_pairs={{16,0},{17,1},{18,2},{19,3},{20,4},{21,5},{22,6},{23,7},{24,8},{25... | collective-permute-start | bytes 245768 | tf_op jit(solution)/shard_map/while/body/eval_jaxpr/ppermute | solution.py:27
  110.2 35.8 %all-to-all-start = ((bf16[16,9,2560]{2,1,0:T(8,128)(2,1)}), bf16[16,9,2560]{2,1,0:T(8,128)(2,1)S(1)}, u32[]{:S(2)}, u32[]{:S(2)}) async-start(bf16[16,9,2560]{2,1,0:T(8,128)(2,1)} %reshape.280), calls=%async_computation | async-start | bytes 2621440 | tf_op jit(solution)/shard_map/while/body/eval_jaxpr/all_to_all | solution.py:105
  115.9 81.3 %collective-permute-start = (bf16[16,2560]{1,0:T(8,128)(2,1)}, bf16[16,2560]{1,0:T(8,128)(2,1)}, u32[]{:S(2)}, u32[]{:S(2)}) collective-permute-start(bf16[16,2560]{1,0:T(8,128)(2,1)} %broadcast_select_fusion.6), channel_id=1, source_target_pairs={{16,0},{17,1},{18,2},{19,3},{20,4},{21,5},{22,6},{23,7},{24,8},{25... | collective-permute-start | bytes 245768 | tf_op jit(solution)/shard_map/while/body/eval_jaxpr/ppermute | solution.py:27
  172.2 9.6 %collective-permute-start.11 = (bf16[1,9,2560]{2,1,0:T(8,128)(2,1)S(1)}, bf16[1,9,2560]{2,1,0:T(8,128)(2,1)S(1)}, u32[]{:S(2)}, u32[]{:S(2)}) collective-permute-start(bf16[1,9,2560]{2,1,0:T(8,128)(2,1)S(1)} %get-tuple-element.718), channel_id=1, source_target_pairs={{0,11},{1,10},{2,9},{3,8},{4,15},{5,14},{6,13},{7,12},{8,3},{9,2},... | collective-permute-start | bytes 138248 | tf_op jit(solution)/shard_map/while/body/eval_jaxpr/ppermute | solution.py:118
  175.0 12.3 %collective-permute-start.12 = (bf16[1,9,2560]{2,1,0:T(8,128)(2,1)S(1)}, bf16[1,9,2560]{2,1,0:T(8,128)(2,1)S(1)}, u32[]{:S(2)}, u32[]{:S(2)}) collective-permute-start(bf16[1,9,2560]{2,1,0:T(8,128)(2,1)S(1)} %get-tuple-element.719), channel_id=1, source_target_pairs={{0,12},{1,13},{2,14},{3,15},{4,8},{5,9},{6,10},{7,11},{8,4},{9,5},... | collective-permute-start | bytes 138248 | tf_op jit(solution)/shard_map/while/body/eval_jaxpr/ppermute | solution.py:118
  178.5 13.8 %collective-permute-start.13 = (bf16[1,9,2560]{2,1,0:T(8,128)(2,1)S(1)}, bf16[1,9,2560]{2,1,0:T(8,128)(2,1)S(1)}, u32[]{:S(2)}, u32[]{:S(2)}) collective-permute-start(bf16[1,9,2560]{2,1,0:T(8,128)(2,1)S(1)} %get-tuple-element.720), channel_id=1, source_target_pairs={{0,13},{1,12},{2,15},{3,14},{4,9},{5,8},{6,11},{7,10},{8,5},{9,4},... | collective-permute-start | bytes 138248 | tf_op jit(solution)/shard_map/while/body/eval_jaxpr/ppermute | solution.py:118
  181.7 13.1 %collective-permute-start.14 = (bf16[1,9,2560]{2,1,0:T(8,128)(2,1)S(1)}, bf16[1,9,2560]{2,1,0:T(8,128)(2,1)S(1)}, u32[]{:S(2)}, u32[]{:S(2)}) collective-permute-start(bf16[1,9,2560]{2,1,0:T(8,128)(2,1)S(1)} %get-tuple-element.721), channel_id=1, source_target_pairs={{0,14},{1,15},{2,12},{3,13},{4,10},{5,11},{6,8},{7,9},{8,6},{9,7},... | collective-permute-start | bytes 138248 | tf_op jit(solution)/shard_map/while/body/eval_jaxpr/ppermute | solution.py:118
  203.8 95.3 %collective-permute-start.17 = (bf16[16,2560]{1,0:T(8,128)(2,1)S(1)}, bf16[16,2560]{1,0:T(8,128)(2,1)}, u32[]{:S(2)}, u32[]{:S(2)}) collective-permute-start(bf16[16,2560]{1,0:T(8,128)(2,1)S(1)} %copy.58), channel_id=1, source_target_pairs={{16,0},{17,1},{18,2},{19,3},{20,4},{21,5},{22,6},{23,7},{24,8},{25... | collective-permute-start | bytes 245768 | tf_op jit(solution)/shard_map/while/body/eval_jaxpr/ppermute | solution.py:27
  210.9 35.8 %all-to-all-start = ((bf16[16,9,2560]{2,1,0:T(8,128)(2,1)}), bf16[16,9,2560]{2,1,0:T(8,128)(2,1)S(1)}, u32[]{:S(2)}, u32[]{:S(2)}) async-start(bf16[16,9,2560]{2,1,0:T(8,128)(2,1)} %reshape.280), calls=%async_computation | async-start | bytes 2621440 | tf_op jit(solution)/shard_map/while/body/eval_jaxpr/all_to_all | solution.py:105
  216.5 81.3 %collective-permute-start = (bf16[16,2560]{1,0:T(8,128)(2,1)}, bf16[16,2560]{1,0:T(8,128)(2,1)}, u32[]{:S(2)}, u32[]{:S(2)}) collective-permute-start(bf16[16,2560]{1,0:T(8,128)(2,1)} %broadcast_select_fusion.6), channel_id=1, source_target_pairs={{16,0},{17,1},{18,2},{19,3},{20,4},{21,5},{22,6},{23,7},{24,8},{25... | collective-permute-start | bytes 245768 | tf_op jit(solution)/shard_map/while/body/eval_jaxpr/ppermute | solution.py:27
  275.6 12.3 %collective-permute-start.12 = (bf16[1,9,2560]{2,1,0:T(8,128)(2,1)S(1)}, bf16[1,9,2560]{2,1,0:T(8,128)(2,1)S(1)}, u32[]{:S(2)}, u32[]{:S(2)}) collective-permute-start(bf16[1,9,2560]{2,1,0:T(8,128)(2,1)S(1)} %get-tuple-element.719), channel_id=1, source_target_pairs={{0,12},{1,13},{2,14},{3,15},{4,8},{5,9},{6,10},{7,11},{8,4},{9,5},... | collective-permute-start | bytes 138248 | tf_op jit(solution)/shard_map/while/body/eval_jaxpr/ppermute | solution.py:118
  279.1 13.8 %collective-permute-start.13 = (bf16[1,9,2560]{2,1,0:T(8,128)(2,1)S(1)}, bf16[1,9,2560]{2,1,0:T(8,128)(2,1)S(1)}, u32[]{:S(2)}, u32[]{:S(2)}) collective-permute-start(bf16[1,9,2560]{2,1,0:T(8,128)(2,1)S(1)} %get-tuple-element.720), channel_id=1, source_target_pairs={{0,13},{1,12},{2,15},{3,14},{4,9},{5,8},{6,11},{7,10},{8,5},{9,4},... | collective-permute-start | bytes 138248 | tf_op jit(solution)/shard_map/while/body/eval_jaxpr/ppermute | solution.py:118
  282.4 13.2 %collective-permute-start.14 = (bf16[1,9,2560]{2,1,0:T(8,128)(2,1)S(1)}, bf16[1,9,2560]{2,1,0:T(8,128)(2,1)S(1)}, u32[]{:S(2)}, u32[]{:S(2)}) collective-permute-start(bf16[1,9,2560]{2,1,0:T(8,128)(2,1)S(1)} %get-tuple-element.721), channel_id=1, source_target_pairs={{0,14},{1,15},{2,12},{3,13},{4,10},{5,11},{6,8},{7,9},{8,6},{9,7},... | collective-permute-start | bytes 138248 | tf_op jit(solution)/shard_map/while/body/eval_jaxpr/ppermute | solution.py:118
  304.4 94.4 %collective-permute-start.17 = (bf16[16,2560]{1,0:T(8,128)(2,1)S(1)}, bf16[16,2560]{1,0:T(8,128)(2,1)}, u32[]{:S(2)}, u32[]{:S(2)}) collective-permute-start(bf16[16,2560]{1,0:T(8,128)(2,1)S(1)} %copy.58), channel_id=1, source_target_pairs={{16,0},{17,1},{18,2},{19,3},{20,4},{21,5},{22,6},{23,7},{24,8},{25... | collective-permute-start | bytes 245768 | tf_op jit(solution)/shard_map/while/body/eval_jaxpr/ppermute | solution.py:27
  311.5 35.8 %all-to-all-start = ((bf16[16,9,2560]{2,1,0:T(8,128)(2,1)}), bf16[16,9,2560]{2,1,0:T(8,128)(2,1)S(1)}, u32[]{:S(2)}, u32[]{:S(2)}) async-start(bf16[16,9,2560]{2,1,0:T(8,128)(2,1)} %reshape.280), calls=%async_computation | async-start | bytes 2621440 | tf_op jit(solution)/shard_map/while/body/eval_jaxpr/all_to_all | solution.py:105
  317.2 81.3 %collective-permute-start = (bf16[16,2560]{1,0:T(8,128)(2,1)}, bf16[16,2560]{1,0:T(8,128)(2,1)}, u32[]{:S(2)}, u32[]{:S(2)}) collective-permute-start(bf16[16,2560]{1,0:T(8,128)(2,1)} %broadcast_select_fusion.6), channel_id=1, source_target_pairs={{16,0},{17,1},{18,2},{19,3},{20,4},{21,5},{22,6},{23,7},{24,8},{25... | collective-permute-start | bytes 245768 | tf_op jit(solution)/shard_map/while/body/eval_jaxpr/ppermute | solution.py:27
  376.3 12.3 %collective-permute-start.12 = (bf16[1,9,2560]{2,1,0:T(8,128)(2,1)S(1)}, bf16[1,9,2560]{2,1,0:T(8,128)(2,1)S(1)}, u32[]{:S(2)}, u32[]{:S(2)}) collective-permute-start(bf16[1,9,2560]{2,1,0:T(8,128)(2,1)S(1)} %get-tuple-element.719), channel_id=1, source_target_pairs={{0,12},{1,13},{2,14},{3,15},{4,8},{5,9},{6,10},{7,11},{8,4},{9,5},... | collective-permute-start | bytes 138248 | tf_op jit(solution)/shard_map/while/body/eval_jaxpr/ppermute | solution.py:118
  379.8 13.8 %collective-permute-start.13 = (bf16[1,9,2560]{2,1,0:T(8,128)(2,1)S(1)}, bf16[1,9,2560]{2,1,0:T(8,128)(2,1)S(1)}, u32[]{:S(2)}, u32[]{:S(2)}) collective-permute-start(bf16[1,9,2560]{2,1,0:T(8,128)(2,1)S(1)} %get-tuple-element.720), channel_id=1, source_target_pairs={{0,13},{1,12},{2,15},{3,14},{4,9},{5,8},{6,11},{7,10},{8,5},{9,4},... | collective-permute-start | bytes 138248 | tf_op jit(solution)/shard_map/while/body/eval_jaxpr/ppermute | solution.py:118
  383.0 13.2 %collective-permute-start.14 = (bf16[1,9,2560]{2,1,0:T(8,128)(2,1)S(1)}, bf16[1,9,2560]{2,1,0:T(8,128)(2,1)S(1)}, u32[]{:S(2)}, u32[]{:S(2)}) collective-permute-start(bf16[1,9,2560]{2,1,0:T(8,128)(2,1)S(1)} %get-tuple-element.721), channel_id=1, source_target_pairs={{0,14},{1,15},{2,12},{3,13},{4,10},{5,11},{6,8},{7,9},{8,6},{9,7},... | collective-permute-start | bytes 138248 | tf_op jit(solution)/shard_map/while/body/eval_jaxpr/ppermute | solution.py:118
  404.2 94.4 %collective-permute-start.17 = (bf16[16,2560]{1,0:T(8,128)(2,1)S(1)}, bf16[16,2560]{1,0:T(8,128)(2,1)}, u32[]{:S(2)}, u32[]{:S(2)}) collective-permute-start(bf16[16,2560]{1,0:T(8,128)(2,1)S(1)} %copy.58), channel_id=1, source_target_pairs={{16,0},{17,1},{18,2},{19,3},{20,4},{21,5},{22,6},{23,7},{24,8},{25... | collective-permute-start | bytes 245768 | tf_op jit(solution)/shard_map/while/body/eval_jaxpr/ppermute | solution.py:27
  411.3 35.8 %all-to-all-start = ((bf16[16,9,2560]{2,1,0:T(8,128)(2,1)}), bf16[16,9,2560]{2,1,0:T(8,128)(2,1)S(1)}, u32[]{:S(2)}, u32[]{:S(2)}) async-start(bf16[16,9,2560]{2,1,0:T(8,128)(2,1)} %reshape.280), calls=%async_computation | async-start | bytes 2621440 | tf_op jit(solution)/shard_map/while/body/eval_jaxpr/all_to_all | solution.py:105
  417.0 81.3 %collective-permute-start = (bf16[16,2560]{1,0:T(8,128)(2,1)}, bf16[16,2560]{1,0:T(8,128)(2,1)}, u32[]{:S(2)}, u32[]{:S(2)}) collective-permute-start(bf16[16,2560]{1,0:T(8,128)(2,1)} %broadcast_select_fusion.6), channel_id=1, source_target_pairs={{16,0},{17,1},{18,2},{19,3},{20,4},{21,5},{22,6},{23,7},{24,8},{25... | collective-permute-start | bytes 245768 | tf_op jit(solution)/shard_map/while/body/eval_jaxpr/ppermute | solution.py:27
  476.1 12.3 %collective-permute-start.12 = (bf16[1,9,2560]{2,1,0:T(8,128)(2,1)S(1)}, bf16[1,9,2560]{2,1,0:T(8,128)(2,1)S(1)}, u32[]{:S(2)}, u32[]{:S(2)}) collective-permute-start(bf16[1,9,2560]{2,1,0:T(8,128)(2,1)S(1)} %get-tuple-element.719), channel_id=1, source_target_pairs={{0,12},{1,13},{2,14},{3,15},{4,8},{5,9},{6,10},{7,11},{8,4},{9,5},... | collective-permute-start | bytes 138248 | tf_op jit(solution)/shard_map/while/body/eval_jaxpr/ppermute | solution.py:118
  479.6 13.8 %collective-permute-start.13 = (bf16[1,9,2560]{2,1,0:T(8,128)(2,1)S(1)}, bf16[1,9,2560]{2,1,0:T(8,128)(2,1)S(1)}, u32[]{:S(2)}, u32[]{:S(2)}) collective-permute-start(bf16[1,9,2560]{2,1,0:T(8,128)(2,1)S(1)} %get-tuple-element.720), channel_id=1, source_target_pairs={{0,13},{1,12},{2,15},{3,14},{4,9},{5,8},{6,11},{7,10},{8,5},{9,4},... | collective-permute-start | bytes 138248 | tf_op jit(solution)/shard_map/while/body/eval_jaxpr/ppermute | solution.py:118
  482.8 13.2 %collective-permute-start.14 = (bf16[1,9,2560]{2,1,0:T(8,128)(2,1)S(1)}, bf16[1,9,2560]{2,1,0:T(8,128)(2,1)S(1)}, u32[]{:S(2)}, u32[]{:S(2)}) collective-permute-start(bf16[1,9,2560]{2,1,0:T(8,128)(2,1)S(1)} %get-tuple-element.721), channel_id=1, source_target_pairs={{0,14},{1,15},{2,12},{3,13},{4,10},{5,11},{6,8},{7,9},{8,6},{9,7},... | collective-permute-start | bytes 138248 | tf_op jit(solution)/shard_map/while/body/eval_jaxpr/ppermute | solution.py:118
  (69 other events, 434.6 us)
